TPU v7x, 512 devices: a whole 4x8x8 slice. The times are simulated.
512 devices in a mesh: req: 64 (over x, z, core), wt: 8 (over y).
Axes of the slice: x: 4, y: 8, z: 8, core: 2. Of those that a mesh axis runs over, the one named last changes fastest.
Arguments:
- streams: bfloat16 [4, 32768, 2048], P(None, 'req', 'wt'), may hold values from -6 to 6
- doc_ids: int32 [64, 512], P('req'), may hold values from 0 to 3, never falling along the last dimension, each value on 1 to 256 neighbouring positions
- doc_adapter: int32 [64, 4, 1], P('req'), may hold values from 0 to 15
- width_weights: float32 [4], replicated, may hold values from 0.2 to 1
- stream_mixing: float32 [4, 4], replicated, may hold values from -3 to 3
- depth_static: float32 [4], replicated, may hold values from 0.2 to 1
- depth_dir: bfloat16 [2048, 4], replicated, may hold values from -0.125 to 0.125
- qkv_weight: bfloat16 [2048, 3, 2048], P('req', None, 'wt')
- adapter_down: bfloat16 [16, 2048, 16], P('wt'), may hold values from -0.125 to 0.125
- adapter_up: bfloat16 [16, 16, 3, 2048], P(None, None, None, 'wt'), may hold values from -1.5 to 1.5
- out_weight: bfloat16 [2048, 2048], P('req', 'wt'), may hold values from -0.125 to 0.125
- page_slot: int32 [2048], P('req'), may hold values from 0 to 2047, as said below
Outputs:
- new_streams: bfloat16 [4, 32768, 2048], P(None, 'req', 'wt')
- kv_pool: bfloat16 [2048, 16, 2, 2048], P('req', None, None, 'wt')
Inputs may be any that keep to these rules, and one draw needn't show every extreme that they name: page_slot is a permutation of all page slots; page p lands on index page_slot[p] // 32 of req; the pages 2k and 2k + 1 form one request and land on the same index; of the pages of one index of req at most 2 land on any one index, and exactly 2 on some.
All inputs are finite; a program needn't handle non-finite values.
Results may differ from a plain program's by a relative error of at most 0.008.
Values may be sent and summed in bfloat16 or wider, within the bound.
A program may use at most 64 MiB of HBM per device.

v0:
```python
import math
import jax
import jax.numpy as jnp
from jax import lax
from jax.sharding import PartitionSpec as P

HD = 128
R = 16
PAGE = 16
EPSILON = 1e-05


def body(
    streams,
    doc_ids,
    doc_adapter,
    width_weights,
    stream_mixing,
    depth_static,
    depth_dir,
    qkv_weight,
    adapter_down,
    adapter_up,
    out_weight,
    page_slot,
):
    count_streams = streams.shape[0]
    tokens = streams.shape[1]
    mixed_local = width_weights[0] * streams[0].astype(jnp.float32)
    for stream in range(1, count_streams):
        mixed_local = mixed_local + width_weights[stream] * streams[stream].astype(jnp.float32)
    gathered = lax.all_gather(mixed_local.astype(jnp.bfloat16), "wt", axis=1, tiled=True)
    widened = gathered.astype(jnp.float32)
    normed = (
        widened * lax.rsqrt(jnp.mean(widened * widened, axis=-1, keepdims=True) + EPSILON)
    ).astype(jnp.bfloat16)
    segment = doc_ids[0]
    doc_table = doc_adapter[0, :, 0]
    token_adapter = jnp.sum(
        jnp.where(
            segment[:, None] == jnp.arange(doc_table.shape[0])[None, :], doc_table[None, :], 0
        ),
        axis=1,
    )
    adapters_total = adapter_up.shape[0]
    selector = (token_adapter[:, None] == jnp.arange(adapters_total)[None, :]).astype(jnp.float32)
    every_rank = jnp.einsum(
        "td,adr->tar",
        normed,
        lax.all_gather(adapter_down, "wt", axis=0, tiled=True),
        preferred_element_type=jnp.float32,
    )
    shrunk = jnp.sum(selector[:, :, None] * every_rank, axis=1)
    shrunk = shrunk.astype(jnp.bfloat16)
    spread = (
        (selector[:, :, None] * shrunk.astype(jnp.float32)[:, None, :])
        .reshape(tokens, adapters_total * R)
        .astype(jnp.bfloat16)
    )
    lowrank = jnp.dot(
        spread, adapter_up.reshape(adapters_total * R, -1), preferred_element_type=jnp.float32
    )
    width_local = qkv_weight.shape[2]
    portion = lax.all_gather(qkv_weight, "req", axis=0, tiled=True)
    base = jnp.dot(
        normed, portion.reshape(portion.shape[0], -1), preferred_element_type=jnp.float32
    )
    heads_local = width_local // HD
    projected = (base + lowrank).astype(jnp.bfloat16).reshape(tokens, 3, heads_local, HD)
    key_rows = projected[:, 1]
    value_rows = projected[:, 2]
    block_rows = min(512, tokens)
    blocks = tokens // block_rows
    positions = jnp.arange(tokens)

    def attend(packed):
        query_block, query_pos, query_seg = packed
        scores = jnp.einsum(
            "qhd,khd->hqk", query_block, key_rows, preferred_element_type=jnp.float32
        ) / math.sqrt(HD)
        allowed = (query_seg[:, None] == segment[None, :]) & (
            positions[None, :] <= query_pos[:, None]
        )
        scores = jnp.where(allowed[None], scores, -1e30)
        highest = jnp.max(scores, axis=-1, keepdims=True)
        weights = jnp.exp(scores - highest)
        weights = (weights / jnp.sum(weights, axis=-1, keepdims=True)).astype(jnp.bfloat16)
        return jnp.einsum(
            "hqk,khd->qhd", weights, value_rows, preferred_element_type=jnp.float32
        ).astype(jnp.bfloat16)

    attended = lax.map(
        attend,
        (
            projected[:, 0].reshape(blocks, block_rows, heads_local, HD),
            positions.reshape(blocks, block_rows),
            segment.reshape(blocks, block_rows),
        ),
    )
    attended = attended.reshape(tokens, width_local)
    every_row = lax.all_gather(out_weight, "req", axis=0, tiled=True)
    own_rows = lax.all_to_all(every_row, "wt", split_axis=0, concat_axis=1, tiled=True)
    layer_out = lax.psum_scatter(
        jnp.dot(attended, own_rows, preferred_element_type=jnp.float32).astype(jnp.bfloat16),
        "wt",
        scatter_dimension=1,
        tiled=True,
    ).astype(jnp.float32)
    depth = depth_static[None, :] + jnp.tanh(
        jnp.dot(normed, depth_dir, preferred_element_type=jnp.float32)
    )
    outputs = []
    for stream in range(count_streams):
        carried = stream_mixing[stream, 0] * streams[0].astype(jnp.float32)
        for source in range(1, count_streams):
            carried = carried + stream_mixing[stream, source] * streams[source].astype(jnp.float32)
        outputs.append((carried + depth[:, stream][:, None] * layer_out).astype(jnp.bfloat16))
    new_streams = jnp.stack(outputs)
    page_count = page_slot.shape[0]
    cache = projected[:, 1:3].reshape(page_count, PAGE, 2, width_local)
    groups = lax.axis_size("req")
    capacity = 2 * max(1, page_count // (2 * groups))
    target_dev = page_slot // page_count
    local_slot = page_slot % page_count
    ordinal = jnp.arange(page_count)
    earlier = (target_dev[None, :] == target_dev[:, None]) & (ordinal[None, :] < ordinal[:, None])
    placement = target_dev * capacity + jnp.sum(earlier.astype(jnp.int32), axis=1)
    outgoing = (
        jnp.zeros((groups * capacity, PAGE, 2, width_local), jnp.bfloat16).at[placement].set(cache)
    )
    labels = (
        jnp.full((groups * capacity,), -1.0, jnp.bfloat16)
        .at[placement]
        .set(local_slot.astype(jnp.bfloat16))
    )
    incoming, arrived = (
        lax.all_to_all(outgoing, "req", split_axis=0, concat_axis=0, tiled=True),
        lax.all_to_all(labels, "req", split_axis=0, concat_axis=0, tiled=True),
    )
    slot_index = arrived.astype(jnp.int32)
    slot_index = jnp.where(slot_index < 0, page_count, slot_index)
    kv_pool = (
        jnp.zeros((page_count + 1, PAGE, 2, width_local), jnp.bfloat16)
        .at[slot_index]
        .set(incoming)[:page_count]
    )
    return (new_streams, kv_pool)


def solution(mesh):
    in_specs = (
        P(None, "req", "wt"),
        P("req", None),
        P("req", None, None),
        P(),
        P(),
        P(),
        P(),
        P("req", None, "wt"),
        P("wt", None, None),
        P(None, None, None, "wt"),
        P("req", "wt"),
        P("req"),
    )
    out_specs = (P(None, "req", "wt"), P("req", None, None, "wt"))
    return jax.shard_map(body, mesh=mesh, in_specs=in_specs, out_specs=out_specs, check_vma=False)
```

profile of v0, /device:TPU:1, one launch (start us, length us, event | category | flops | bytes accessed | tf_op | source)
XLA Modules:
  0.0 408.4 jit_solution(16914693759775817778)
XLA Ops:
  8.0 1.5 fusion.59
  9.4 4.6 %fusion.24 = bf16[1,512,256]{2,1,0:T(8,128)(2,1)} fusion(f32[]{:T(128)} %bitcast.8, f32[]{:T(128)} %bitcast.7, f32[]{:T(128)} %bitcast.6, f32[]{:T(128)} %bitcast.5, bf16[4,512,256]{2,1,0:T(8,128)(2,1)} %param.12), kind=kLoop, calls=%fused_computation.62 | loop fusion | flops 1572864 | bytes 1310736 | tf_op jit(solution)/shard_map/convert_element_type | solution.py:32
  15.4 84.8 %all-gather.10.cloned.1.call-done = bf16[2048,256]{1,0:T(8,128)(2,1)} async-done(((bf16[32,256]{1,0:T(8,128)(2,1)}), bf16[2048,256]{1,0:T(8,128)(2,1)}) %all-gather.10.cloned.1.call-update) | async-done | bytes 1048592 | tf_op jit(solution)/shard_map/all_gather | solution.py:101
  100.2 6.5 %all-to-all-start = ((bf16[8,256,256]{2,1,0:T(8,128)(2,1)}), bf16[8,256,256]{2,1,0:T(8,128)(2,1)S(1)}, u32[]{:S(2)}, u32[]{:S(2)}) async-start(bf16[8,256,256]{2,1,0:T(8,128)(2,1)} %bitcast.120), calls=%async_computation | async-start | bytes 2097152 | tf_op jit(solution)/shard_map/all_to_all | solution.py:102
  109.9 50.0 %all-gather.12.cloned.1.call-done = bf16[1,512,2048]{2,1,0:T(8,128)(2,1)} async-done(((bf16[1,512,256]{2,1,0:T(8,128)(2,1)}), bf16[1,512,2048]{2,1,0:T(8,128)(2,1)}) %all-gather.12.cloned.1.call-update) | async-done | bytes 2097168 | tf_op jit(solution)/shard_map/all_gather | solution.py:32
  159.9 2.2 fusion.1
  162.8 34.9 %all-gather.8.cloned.1.call-done = bf16[16,2048,16]{1,2,0:T(8,128)(2,1)} async-done(((bf16[2,2048,16]{1,2,0:T(8,128)(2,1)}), bf16[16,2048,16]{1,2,0:T(8,128)(2,1)}) %all-gather.8.cloned.1.call-update) | async-done | bytes 1048592 | tf_op jit(solution)/shard_map/all_gather | solution.py:50
  197.7 2.1 fusion.51
  200.4 88.9 %all-gather.6.cloned.1.call-done = bf16[2048,3,256]{2,0,1:T(8,128)(2,1)} async-done(((bf16[32,3,256]{2,0,1:T(8,128)(2,1)}), bf16[2048,3,256]{2,0,1:T(8,128)(2,1)}) %all-gather.6.cloned.1.call-update) | async-done | bytes 3145744 | tf_op jit(solution)/shard_map/all_gather | solution.py:64
  289.4 4.7 %copy.49 = bf16[2048,3,256]{0,2,1:T(8,128)(2,1)} copy(bf16[2048,3,256]{2,0,1:T(8,128)(2,1)} %all-gather.6.cloned.1.call-done) | data formatting | bytes 6291456 | tf_op jit(solution)/shard_map/all_gather | solution.py:64
  294.1 4.4 %fusion.53 = f32[512,768]{1,0:T(8,128)S(1)} fusion(bf16[2048,768]{0,1:T(8,128)(2,1)} %bitcast.116, bf16[1,512,2048]{2,1,0:T(8,128)(2,1)} %all-gather.12.cloned.1.call-done, f32[512]{0:T(512)S(1)} %copy-done.9), kind=kOutput, calls=%fused_computation.110 | convolution fusion | flops 1613758464 | bytes 6817792 | tf_op jit(solution)/shard_map/dot_general | solution.py:65
  299.9 2.3 fusion.60
  302.1 1.9 convolution_convert_fusion.1
  304.1 2.1 convolution_convert_fusion
  307.9 6.3 %all-to-all-start.1 = ((bf16[64,2,1]{1,2,0:T(2,128)(2,1)}), bf16[64,2,1]{1,2,0:T(2,128)(2,1)S(1)}, u32[]{:S(2)}, u32[]{:S(2)}) async-start(bf16[64,2,1]{1,2,0:T(2,128)(2,1)} %all_to_all.30), calls=%async_computation.2 | async-start | bytes 65536 | tf_op jit(solution)/shard_map/all_to_all | solution.py:138
  315.0 1.6 broadcast_in_dim.85
  316.6 4.3 %scatter_fusion = bf16[128,16,2,256]{3,1,2,0:T(8,128)(2,1)} fusion(bf16[128,16,2,256]{3,1,2,0:T(8,128)(2,1)} %broadcast_in_dim.85, s32[32]{0:T(128)S(1)} %compare_select_fusion.2, bf16[32,16,2,256]{3,1,2,0:T(8,128)(2,1)S(1)} %copy.58), kind=kCustom, calls=%fused_computation.1 | custom fusion | bytes 1572992 | tf_op jit(solution)/shard_map/scatter | solution.py:129
  321.0 2.5 all-to-all-done.1
  323.5 8.1 %all-to-all-start.2 = ((bf16[128,16,2,256]{3,1,2,0:T(8,128)(2,1)}), bf16[128,16,2,256]{3,1,2,0:T(8,128)(2,1)S(1)}, u32[]{:S(2)}, u32[]{:S(2)}) async-start(bf16[128,16,2,256]{3,1,2,0:T(8,128)(2,1)} %scatter_fusion), calls=%async_computation.3 | async-start | bytes 4194304 | tf_op jit(solution)/shard_map/all_to_all | solution.py:137
  332.6 2.3 fusion.4
  334.9 47.8 %all-to-all-done.2 = bf16[128,16,2,256]{3,1,2,0:T(8,128)(2,1)S(1)} async-done(((bf16[128,16,2,256]{3,1,2,0:T(8,128)(2,1)}), bf16[128,16,2,256]{3,1,2,0:T(8,128)(2,1)S(1)}, u32[]{:S(2)}, u32[]{:S(2)}) %all-to-all-start.2) | async-done | bytes 2097184 | tf_op jit(solution)/shard_map/all_to_all | solution.py:137
  382.8 4.6 %scatter_fusion.1 = bf16[33,16,2,256]{3,1,2,0:T(8,128)(2,1)S(1)} fusion(bf16[33,16,2,256]{3,1,2,0:T(8,128)(2,1)S(1)} %broadcast_in_dim.81, s32[128]{0:T(128)S(1)} %fusion.46, bf16[128,16,2,256]{3,1,2,0:T(8,128)(2,1)S(1)} %all-to-all-done.2), kind=kCustom, calls=%fused_computation.2 | custom fusion | bytes 6291968 | tf_op jit(solution)/shard_map/scatter | solution.py:145
  388.8 6.4 %fusion.40 = (bf16[1,512,256]{2,1,0:T(8,128)(2,1)S(1)}, bf16[1,512,256]{2,1,0:T(8,128)(2,1)S(1)}) fusion(bf16[512,256]{1,0:T(8,128)(2,1)} %reduce-scatter.2.cloned.1.call-done, f32[512]{0:T(512)S(1)} %bitcast.128, f32[]{:T(128)} %bitcast.38, f32[]{:T(128)} %bitcast.37, f32[]{:T(128)} %bitcast.36, f32[]{:T(128)} %bitcast.35, ...), kind=kLoop, calls=%fused_computation.82 | loop fusion | flops 3276800 | bytes 1839136 | tf_op jit(solution)/shard_map/stack | solution.py:118
  395.3 5.5 %fusion.42 = (bf16[1,512,256]{2,1,0:T(8,128)(2,1)S(1)}, bf16[1,512,256]{2,1,0:T(8,128)(2,1)S(1)}) fusion(bf16[512,256]{1,0:T(8,128)(2,1)S(1)} %copy-done.3, f32[512]{0:T(512)S(1)} %bitcast.125, f32[]{:T(128)} %bitcast.3, f32[]{:T(128)} %bitcast.2, f32[]{:T(128)} %bitcast.1, f32[]{:T(128)} %bitcast, bf16[4,512,256]{2,1,0:T(8,128)(2,1)S(1)} %copy-done.1, ...), kind=kLoop, calls=%fused_computation.84 | loop fusion | flops 3276800 | bytes 1839136 | tf_op jit(solution)/shard_map/stack | solution.py:118
  (77 shorter events, 13.9 us)
Async XLA Ops:
  7.2 325.4 %copy-start = (bf16[2048,4]{0,1:T(4,128)(2,1)S(1)}, bf16[2048,4]{0,1:T(4,128)(2,1)}, u32[]{:S(2)}) copy-start(bf16[2048,4]{0,1:T(4,128)(2,1)} %param.18) | copy-start | bytes 49156
  7.2 99.5 %copy-start.12 = (s32[32]{0:T(128)S(1)}, s32[32]{0:T(128)}, u32[]{:S(2)}) copy-start(s32[32]{0:T(128)} %param.23) | copy-start | bytes 388
  7.2 100.0 %copy-start.4 = (bf16[16,16,3,256]{3,1,2,0:T(8,128)(2,1)S(1)}, bf16[16,16,3,256]{3,1,2,0:T(8,128)(2,1)}, u32[]{:S(2)}) copy-start(bf16[16,16,3,256]{3,1,2,0:T(8,128)(2,1)} %param.21) | copy-start | bytes 1179652
  7.2 93.0 %all-gather.10.cloned.1.call-start = ((), (), s32[]{:S(2)}) async-start(), calls=%async_computation.6 | async-start | bytes 1064960 | tf_op jit(solution)/shard_map/all_gather | solution.py:101
  7.9 152.0 %all-gather.12.cloned.1.call-start = ((), (), s32[]{:S(2)}) async-start(), calls=%async_computation.8 | async-start | bytes 2359296 | tf_op jit(solution)/shard_map/all_gather | solution.py:32
  14.1 94.2 %copy-start.8 = (s32[1,512]{1,0:T(1,128)S(1)}, s32[1,512]{1,0:T(1,128)}, u32[]{:S(2)}) copy-start(s32[1,512]{1,0:T(1,128)} %param.13) | copy-start | bytes 6148
  14.1 94.2 %copy-start.11 = (s32[1,4,1]{1,2,0:T(1,128)S(1)}, s32[1,4,1]{1,2,0:T(1,128)}, u32[]{:S(2)}) copy-start(s32[1,4,1]{1,2,0:T(1,128)} %param.14) | copy-start | bytes 52
  14.1 183.6 %all-gather.8.cloned.1.call-start = ((), (), s32[]{:S(2)}) async-start(), calls=%async_computation.5 | async-start | bytes 1179648 | tf_op jit(solution)/shard_map/all_gather | solution.py:50
  14.8 274.5 %all-gather.6.cloned.1.call-start = ((), (), s32[]{:S(2)}) async-start(), calls=%async_computation.4 | async-start | bytes 3194880 | tf_op jit(solution)/shard_map/all_gather | solution.py:64
  100.2 99.7 %all-to-all-start = ((bf16[8,256,256]{2,1,0:T(8,128)(2,1)}), bf16[8,256,256]{2,1,0:T(8,128)(2,1)S(1)}, u32[]{:S(2)}, u32[]{:S(2)}) async-start(bf16[8,256,256]{2,1,0:T(8,128)(2,1)} %bitcast.120), calls=%async_computation | async-start | bytes 2097152 | tf_op jit(solution)/shard_map/all_to_all | solution.py:102
  106.7 282.2 %reduce-scatter.2.cloned.1.call-start = ((), (), s32[]{:S(2)}) async-start(), calls=%async_computation.7 | async-start | bytes 2359296 | tf_op jit(solution)/shard_map/reduce_scatter | solution.py:103
  107.2 1.8 copy-start.14
  159.9 37.7 %copy-start.2 = (bf16[1,512,2048]{2,1,0:T(8,128)(2,1)S(1)}, bf16[1,512,2048]{2,1,0:T(8,128)(2,1)}, u32[]{:S(2)}) copy-start(bf16[1,512,2048]{2,1,0:T(8,128)(2,1)} %all-gather.12.cloned.1.call-done) | copy-start | bytes 6291460
  197.7 2.1 copy-start.5
  200.4 93.7 %copy-start.9 = (f32[512]{0:T(512)S(1)}, f32[512]{0:T(512)}, u32[]{:S(2)}) copy-start(f32[512]{0:T(512)} %add_rsqrt_fusion) | copy-start | bytes 6148
  304.0 2.1 copy-start.15
  304.1 2.1 copy-start.16
  307.9 15.6 %all-to-all-start.1 = ((bf16[64,2,1]{1,2,0:T(2,128)(2,1)}), bf16[64,2,1]{1,2,0:T(2,128)(2,1)S(1)}, u32[]{:S(2)}, u32[]{:S(2)}) async-start(bf16[64,2,1]{1,2,0:T(2,128)(2,1)} %all_to_all.30), calls=%async_computation.2 | async-start | bytes 65536 | tf_op jit(solution)/shard_map/all_to_all | solution.py:138
  321.0 10.6 %copy-start.7 = (f32[4,4]{1,0:T(4,128)S(1)}, f32[4,4]{1,0:T(4,128)}, u32[]{:S(2)}) copy-start(f32[4,4]{1,0:T(4,128)} %param.16) | copy-start | bytes 196
  321.0 11.5 %copy-start.10 = (f32[512]{0:T(512)S(1)}, f32[512]{0:T(512)}, u32[]{:S(2)}) copy-start(f32[512]{0:T(512)} %add_rsqrt_fusion) | copy-start | bytes 6148
  321.0 11.6 %copy-start.13 = (f32[4]{0:T(128)S(1)}, f32[4]{0:T(128)}, u32[]{:S(2)}) copy-start(f32[4]{0:T(128)} %param.17) | copy-start | bytes 52
  323.5 59.3 %all-to-all-start.2 = ((bf16[128,16,2,256]{3,1,2,0:T(8,128)(2,1)}), bf16[128,16,2,256]{3,1,2,0:T(8,128)(2,1)S(1)}, u32[]{:S(2)}, u32[]{:S(2)}) async-start(bf16[128,16,2,256]{3,1,2,0:T(8,128)(2,1)} %scatter_fusion), calls=%async_computation.3 | async-start | bytes 4194304 | tf_op jit(solution)/shard_map/all_to_all | solution.py:137
  387.4 1.4 copy-start.1
  388.8 6.4 %copy-start.3 = (bf16[512,256]{1,0:T(8,128)(2,1)S(1)}, bf16[512,256]{1,0:T(8,128)(2,1)}, u32[]{:S(2)}) copy-start(bf16[512,256]{1,0:T(8,128)(2,1)} %reduce-scatter.2.cloned.1.call-done) | copy-start | bytes 786436
  (1 other events, 1.0 us)
Sparse Core Ops, SparseCore 0:
  11.4 88.7 all-gather.9
  102.8 57.1 all-gather.11
  162.0 35.5 all-gather.7
  200.9 88.4 all-gather.5
  306.3 37.3 reduce-scatter.1
where the time goes:
time: 409 us; the launch traced here: 408 us
  waiting for transfers between devices  311 us (76%)
  other arithmetic  23.5 us (6%)
  local copies, waits for them, and re-layouts  23.4 us (6%)
  starting transfers between devices  21 us (5%)
  matrix products  15.4 us (4%)
  between operations  14.1 us (3%)
    all_gather x1, waiting for transfers between devices, body(): portion = lax.all_gather(qkv_weight, 'req', axis=0, tiled=True)  88.9 us
    all_gather x1, waiting for transfers between devices, body(): every_row = lax.all_gather(out_weight, 'req', axis=0, tiled=True)  84.8 us
    all_gather x1, waiting for transfers between devices, body(): lax.all_gather(mixed_local.astype(jnp.bfloat16), 'wt', axis=1, tiled=True)  50 us
    all_to_all x1, waiting for transfers between devices, body(): lax.all_to_all(outgoing, 'req', split_axis=0, concat_axis=0, tiled=True)  47.8 us
    all_gather x1, waiting for transfers between devices, body(): lax.all_gather(adapter_down, 'wt', axis=0, tiled=True)  34.9 us
    another operation x3, other arithmetic, body(): new_streams = jnp.stack(outputs)  13 us
  transfers between devices with their start and end apart: 8, of which 6 were waited for; matrix products, arithmetic and copies ran while one was open for 8% of the time, Pallas kernels for 0%

commit v1 on v0

--- a/solution.py
+++ b/solution.py
@@ -1,13 +1,25 @@
+import functools
 import math
 import jax
 import jax.numpy as jnp
 from jax import lax
 from jax.sharding import PartitionSpec as P
+from jax.lax import all_to_all, axis_size
 
 HD = 128
 R = 16
 PAGE = 16
 EPSILON = 1e-05
+
+
+def answer_panel(xin, a_name):
+    n_slots = axis_size(a_name)
+    vals = [n_slots if dd == 0 else 1 for dd in range(xin.ndim)]
+    part_next = jnp.tile(xin, vals)
+    return all_to_all(part_next, a_name, split_axis=0, concat_axis=0, tiled=True)
+
+
+clusters_track = functools.partial(answer_panel, a_name="wt")
 
 
 def body(
@@ -45,10 +57,7 @@
     adapters_total = adapter_up.shape[0]
     selector = (token_adapter[:, None] == jnp.arange(adapters_total)[None, :]).astype(jnp.float32)
     every_rank = jnp.einsum(
-        "td,adr->tar",
-        normed,
-        lax.all_gather(adapter_down, "wt", axis=0, tiled=True),
-        preferred_element_type=jnp.float32,
+        "td,adr->tar", normed, clusters_track(adapter_down), preferred_element_type=jnp.float32
     )
     shrunk = jnp.sum(selector[:, :, None] * every_rank, axis=1)
     shrunk = shrunk.astype(jnp.bfloat16)

time: 409 us -> 367 us (0.90)
  waiting for transfers between devices: 311 us -> 237 us
  blocking collectives: 0 us -> 33.6 us
    all_gather x1 -> x0, waiting for transfers between devices: 34.9 us -> none  [body(): lax.all_gather(adapter_down, 'wt', axis=0, tiled=True)]
    all_gather x1, waiting for transfers between devices: 84.8 us -> 50.8 us  [body(): every_row = lax.all_gather(out_weight, 'req', axis=0, tiled=True)]
    all_to_all x0 -> x1, blocking collectives: none -> 33.6 us  [answer_panel(): all_to_all(part_next, a_name, split_axis=0, concat_axis=0, tiled=True)]
    all_gather x1, waiting for transfers between devices: 88.9 us -> 83.9 us  [body(): portion = lax.all_gather(qkv_weight, 'req', axis=0, tiled=True)]
  transfers between devices with their start and end apart: 8 -> 7, of which waited for: 6 -> 5; matrix products, arithmetic and copies ran while one was open for 8% -> 8% of each run, Pallas kernels for 0% -> 0%
where the time goes in v1:
time: 367 us; the launch traced here: 366 us
  waiting for transfers between devices  237 us (65%)
  blocking collectives  33.6 us (9%)
  local copies, waits for them, and re-layouts  24.3 us (7%)
  other arithmetic  22.2 us (6%)
  starting transfers between devices  21 us (6%)
  matrix products  14.3 us (4%)
  between operations  14.1 us (4%)
    all_gather x1, waiting for transfers between devices, body(): portion = lax.all_gather(qkv_weight, 'req', axis=0, tiled=True)  83.9 us
    all_gather x1, waiting for transfers between devices, body(): every_row = lax.all_gather(out_weight, 'req', axis=0, tiled=True)  50.8 us
    all_gather x1, waiting for transfers between devices, body(): lax.all_gather(mixed_local.astype(jnp.bfloat16), 'wt', axis=1, tiled=True)  50.5 us
    all_to_all x1, waiting for transfers between devices, body(): lax.all_to_all(outgoing, 'req', split_axis=0, concat_axis=0, tiled=True)  47.8 us
    all_to_all x1, blocking collectives, answer_panel(): all_to_all(part_next, a_name, split_axis=0, concat_axis=0, tiled=True)  33.6 us
    another operation x3, other arithmetic, body(): new_streams = jnp.stack(outputs)  12.9 us
    all_to_all x1, starting transfers between devices, body(): lax.all_to_all(outgoing, 'req', split_axis=0, concat_axis=0, tiled=True)  8.03 us
  transfers between devices with their start and end apart: 7, of which 5 were waited for; matrix products, arithmetic and copies ran while one was open for 8% of the time, Pallas kernels for 0%

profile of v1, /device:TPU:1, one launch (start us, length us, event | category | flops | bytes accessed | tf_op | source)
XLA Modules:
  0.0 366.5 jit_solution(3696277062531773913)
XLA Ops:
  8.0 1.4 fusion.59
  9.4 4.6 %fusion.24 = bf16[1,512,256]{2,1,0:T(8,128)(2,1)} fusion(f32[]{:T(128)} %bitcast.8, f32[]{:T(128)} %bitcast.7, f32[]{:T(128)} %bitcast.6, f32[]{:T(128)} %bitcast.5, bf16[4,512,256]{2,1,0:T(8,128)(2,1)} %param.12), kind=kLoop, calls=%fused_computation.62 | loop fusion | flops 1572864 | bytes 1310736 | tf_op jit(solution)/shard_map/convert_element_type | solution.py:44
  15.8 33.6 %all_to_all.39 = bf16[16,2048,16]{1,2,0:T(8,128)(2,1)S(1)} all-to-all(bf16[16,2048,16]{1,2,0:T(8,128)(2,1)S(1)} %bitcast.117), channel_id=1, replica_groups=mesh['req'=64,'wt'=8] {'wt'}, dimensions={0} | all-to-all | bytes 2097152 | tf_op jit(solution)/shard_map/all_to_all | solution.py:19
  49.4 50.8 %all-gather.7.cloned.1.call-done = bf16[2048,256]{1,0:T(8,128)(2,1)} async-done(((bf16[32,256]{1,0:T(8,128)(2,1)}), bf16[2048,256]{1,0:T(8,128)(2,1)}) %all-gather.7.cloned.1.call-update) | async-done | bytes 1048592 | tf_op jit(solution)/shard_map/all_gather | solution.py:110
  100.2 6.5 %all-to-all-start.1 = ((bf16[8,256,256]{2,1,0:T(8,128)(2,1)}), bf16[8,256,256]{2,1,0:T(8,128)(2,1)S(1)}, u32[]{:S(2)}, u32[]{:S(2)}) async-start(bf16[8,256,256]{2,1,0:T(8,128)(2,1)} %bitcast.122), calls=%async_computation.1 | async-start | bytes 2097152 | tf_op jit(solution)/shard_map/all_to_all | solution.py:111
  109.4 50.5 %all-gather.9.cloned.1.call-done = bf16[1,512,2048]{2,1,0:T(8,128)(2,1)} async-done(((bf16[1,512,256]{2,1,0:T(8,128)(2,1)}), bf16[1,512,2048]{2,1,0:T(8,128)(2,1)}) %all-gather.9.cloned.1.call-update) | async-done | bytes 2097168 | tf_op jit(solution)/shard_map/all_gather | solution.py:44
  159.9 2.2 fusion.1
  163.8 83.9 %all-gather.5.cloned.1.call-done = bf16[2048,3,256]{2,0,1:T(8,128)(2,1)} async-done(((bf16[32,3,256]{2,0,1:T(8,128)(2,1)}), bf16[2048,3,256]{2,0,1:T(8,128)(2,1)}) %all-gather.5.cloned.1.call-update) | async-done | bytes 3145744 | tf_op jit(solution)/shard_map/all_gather | solution.py:73
  247.7 4.7 %copy.49 = bf16[2048,3,256]{0,2,1:T(8,128)(2,1)} copy(bf16[2048,3,256]{2,0,1:T(8,128)(2,1)} %all-gather.5.cloned.1.call-done) | data formatting | bytes 6291456 | tf_op jit(solution)/shard_map/all_gather | solution.py:73
  252.4 4.4 %fusion.53 = f32[512,768]{1,0:T(8,128)S(1)} fusion(bf16[2048,768]{0,1:T(8,128)(2,1)} %bitcast.118, bf16[1,512,2048]{2,1,0:T(8,128)(2,1)} %all-gather.9.cloned.1.call-done, f32[512]{0:T(512)S(1)} %add_rsqrt_fusion), kind=kOutput, calls=%fused_computation.110 | convolution fusion | flops 1613758464 | bytes 6817792 | tf_op jit(solution)/shard_map/dot_general | solution.py:74
  258.1 2.3 fusion.60
  260.4 1.9 convolution_convert_fusion.1
  262.3 2.1 convolution_convert_fusion
  266.2 6.3 %all-to-all-start.2 = ((bf16[64,2,1]{1,2,0:T(2,128)(2,1)}), bf16[64,2,1]{1,2,0:T(2,128)(2,1)S(1)}, u32[]{:S(2)}, u32[]{:S(2)}) async-start(bf16[64,2,1]{1,2,0:T(2,128)(2,1)} %all_to_all.34), calls=%async_computation.3 | async-start | bytes 65536 | tf_op jit(solution)/shard_map/all_to_all | solution.py:147
  273.3 1.6 broadcast_in_dim.85
  274.9 4.4 %scatter_fusion = bf16[128,16,2,256]{3,1,2,0:T(8,128)(2,1)} fusion(bf16[128,16,2,256]{3,1,2,0:T(8,128)(2,1)} %broadcast_in_dim.85, s32[32]{0:T(128)S(1)} %compare_select_fusion.2, bf16[32,16,2,256]{3,1,2,0:T(8,128)(2,1)S(1)} %copy.58), kind=kCustom, calls=%fused_computation.1 | custom fusion | bytes 1572992 | tf_op jit(solution)/shard_map/scatter | solution.py:138
  279.2 2.5 all-to-all-done.2
  281.7 8.0 %all-to-all-start.3 = ((bf16[128,16,2,256]{3,1,2,0:T(8,128)(2,1)}), bf16[128,16,2,256]{3,1,2,0:T(8,128)(2,1)S(1)}, u32[]{:S(2)}, u32[]{:S(2)}) async-start(bf16[128,16,2,256]{3,1,2,0:T(8,128)(2,1)} %scatter_fusion), calls=%async_computation.4 | async-start | bytes 4194304 | tf_op jit(solution)/shard_map/all_to_all | solution.py:146
  290.8 2.3 fusion.4
  293.1 47.8 %all-to-all-done.3 = bf16[128,16,2,256]{3,1,2,0:T(8,128)(2,1)S(1)} async-done(((bf16[128,16,2,256]{3,1,2,0:T(8,128)(2,1)}), bf16[128,16,2,256]{3,1,2,0:T(8,128)(2,1)S(1)}, u32[]{:S(2)}, u32[]{:S(2)}) %all-to-all-start.3) | async-done | bytes 2097184 | tf_op jit(solution)/shard_map/all_to_all | solution.py:146
  341.0 4.6 %scatter_fusion.1 = bf16[33,16,2,256]{3,1,2,0:T(8,128)(2,1)S(1)} fusion(bf16[33,16,2,256]{3,1,2,0:T(8,128)(2,1)S(1)} %broadcast_in_dim.81, s32[128]{0:T(128)S(1)} %fusion.46, bf16[128,16,2,256]{3,1,2,0:T(8,128)(2,1)S(1)} %all-to-all-done.3), kind=kCustom, calls=%fused_computation.2 | custom fusion | bytes 6291968 | tf_op jit(solution)/shard_map/scatter | solution.py:154
  345.7 1.3 copy.59
  347.0 6.4 %fusion.40 = (bf16[1,512,256]{2,1,0:T(8,128)(2,1)S(1)}, bf16[1,512,256]{2,1,0:T(8,128)(2,1)S(1)}) fusion(bf16[512,256]{1,0:T(8,128)(2,1)} %reduce-scatter.2.cloned.1.call-done, f32[512]{0:T(512)S(1)} %bitcast.131, f32[]{:T(128)} %bitcast.39, f32[]{:T(128)} %bitcast.38, f32[]{:T(128)} %bitcast.37, f32[]{:T(128)} %bitcast.36, ...), kind=kLoop, calls=%fused_computation.82 | loop fusion | flops 3276800 | bytes 1839136 | tf_op jit(solution)/shard_map/stack | solution.py:127
  353.5 5.3 %fusion.42 = (bf16[1,512,256]{2,1,0:T(8,128)(2,1)S(1)}, bf16[1,512,256]{2,1,0:T(8,128)(2,1)S(1)}) fusion(bf16[512,256]{1,0:T(8,128)(2,1)S(1)} %copy-done.3, f32[512]{0:T(512)S(1)} %bitcast.128, f32[]{:T(128)} %bitcast.3, f32[]{:T(128)} %bitcast.2, f32[]{:T(128)} %bitcast.1, f32[]{:T(128)} %bitcast, bf16[4,512,256]{2,1,0:T(8,128)(2,1)S(1)} %copy-done.1, ...), kind=kLoop, calls=%fused_computation.84 | loop fusion | flops 3276800 | bytes 1839136 | tf_op jit(solution)/shard_map/stack | solution.py:127
  (74 shorter events, 12.9 us)
Async XLA Ops:
  7.2 283.6 %copy-start = (bf16[2048,4]{0,1:T(4,128)(2,1)S(1)}, bf16[2048,4]{0,1:T(4,128)(2,1)}, u32[]{:S(2)}) copy-start(bf16[2048,4]{0,1:T(4,128)(2,1)} %param.18) | copy-start | bytes 49156
  7.2 93.0 %all-gather.7.cloned.1.call-start = ((), (), s32[]{:S(2)}) async-start(), calls=%async_computation.6 | async-start | bytes 1064960 | tf_op jit(solution)/shard_map/all_gather | solution.py:110
  7.9 152.0 %all-gather.9.cloned.1.call-start = ((), (), s32[]{:S(2)}) async-start(), calls=%async_computation.8 | async-start | bytes 2359296 | tf_op jit(solution)/shard_map/all_gather | solution.py:44
  14.0 233.7 %all-gather.5.cloned.1.call-start = ((), (), s32[]{:S(2)}) async-start(), calls=%async_computation.5 | async-start | bytes 3194880 | tf_op jit(solution)/shard_map/all_gather | solution.py:73
  15.7 91.0 %copy-start.11 = (s32[32]{0:T(128)S(1)}, s32[32]{0:T(128)}, u32[]{:S(2)}) copy-start(s32[32]{0:T(128)} %param.23) | copy-start | bytes 388
  15.7 91.6 %copy-start.4 = (bf16[16,16,3,256]{3,1,2,0:T(8,128)(2,1)S(1)}, bf16[16,16,3,256]{3,1,2,0:T(8,128)(2,1)}, u32[]{:S(2)}) copy-start(bf16[16,16,3,256]{3,1,2,0:T(8,128)(2,1)} %param.21) | copy-start | bytes 1179652
  49.4 59.0 %copy-start.7 = (s32[1,512]{1,0:T(1,128)S(1)}, s32[1,512]{1,0:T(1,128)}, u32[]{:S(2)}) copy-start(s32[1,512]{1,0:T(1,128)} %param.13) | copy-start | bytes 6148
  49.4 59.0 %copy-start.10 = (s32[1,4,1]{1,2,0:T(1,128)S(1)}, s32[1,4,1]{1,2,0:T(1,128)}, u32[]{:S(2)}) copy-start(s32[1,4,1]{1,2,0:T(1,128)} %param.14) | copy-start | bytes 52
  100.2 63.1 %all-to-all-start.1 = ((bf16[8,256,256]{2,1,0:T(8,128)(2,1)}), bf16[8,256,256]{2,1,0:T(8,128)(2,1)S(1)}, u32[]{:S(2)}, u32[]{:S(2)}) async-start(bf16[8,256,256]{2,1,0:T(8,128)(2,1)} %bitcast.122), calls=%async_computation.1 | async-start | bytes 2097152 | tf_op jit(solution)/shard_map/all_to_all | solution.py:111
  106.6 240.4 %reduce-scatter.2.cloned.1.call-start = ((), (), s32[]{:S(2)}) async-start(), calls=%async_computation.7 | async-start | bytes 2359296 | tf_op jit(solution)/shard_map/reduce_scatter | solution.py:112
  107.3 1.2 copy-start.13
  159.9 2.2 copy-start.2
  162.2 90.2 %copy-start.8 = (f32[512]{0:T(512)}, f32[512]{0:T(512)S(1)}, u32[]{:S(2)}) copy-start(f32[512]{0:T(512)S(1)} %add_rsqrt_fusion) | copy-start | bytes 6148
  257.2 1.0 copy-start.5
  262.3 2.1 copy-start.14
  262.3 2.1 copy-start.15
  266.2 15.6 %all-to-all-start.2 = ((bf16[64,2,1]{1,2,0:T(2,128)(2,1)}), bf16[64,2,1]{1,2,0:T(2,128)(2,1)S(1)}, u32[]{:S(2)}, u32[]{:S(2)}) async-start(bf16[64,2,1]{1,2,0:T(2,128)(2,1)} %all_to_all.34), calls=%async_computation.3 | async-start | bytes 65536 | tf_op jit(solution)/shard_map/all_to_all | solution.py:147
  279.2 10.5 %copy-start.6 = (f32[4,4]{1,0:T(4,128)S(1)}, f32[4,4]{1,0:T(4,128)}, u32[]{:S(2)}) copy-start(f32[4,4]{1,0:T(4,128)} %param.16) | copy-start | bytes 196
  279.2 11.5 %copy-start.9 = (f32[512]{0:T(512)S(1)}, f32[512]{0:T(512)}, u32[]{:S(2)}) copy-start(f32[512]{0:T(512)} %copy-done.8) | copy-start | bytes 6148
  279.2 11.5 %copy-start.12 = (f32[4]{0:T(128)S(1)}, f32[4]{0:T(128)}, u32[]{:S(2)}) copy-start(f32[4]{0:T(128)} %param.17) | copy-start | bytes 52
  281.7 59.2 %all-to-all-start.3 = ((bf16[128,16,2,256]{3,1,2,0:T(8,128)(2,1)}), bf16[128,16,2,256]{3,1,2,0:T(8,128)(2,1)S(1)}, u32[]{:S(2)}, u32[]{:S(2)}) async-start(bf16[128,16,2,256]{3,1,2,0:T(8,128)(2,1)} %scatter_fusion), calls=%async_computation.4 | async-start | bytes 4194304 | tf_op jit(solution)/shard_map/all_to_all | solution.py:146
  345.7 1.4 copy-start.1
  347.0 6.4 %copy-start.3 = (bf16[512,256]{1,0:T(8,128)(2,1)S(1)}, bf16[512,256]{1,0:T(8,128)(2,1)}, u32[]{:S(2)}) copy-start(bf16[512,256]{1,0:T(8,128)(2,1)} %reduce-scatter.2.cloned.1.call-done) | copy-start | bytes 786436
Sparse Core Ops, SparseCore 0:
  11.3 88.7 all-gather.6
  102.8 57.1 all-gather.8
  163.3 84.2 all-gather.4
  264.6 37.4 reduce-scatter.1
